TPU v7x, 32 devices: a whole 2x2x4 slice. The times are simulated.
32 devices in a mesh: base: 16 (over z, x, core), band: 2 (over y).
Axes of the slice: x: 2, y: 2, z: 4, core: 2. Of those that a mesh axis runs over, the one named last changes fastest.
Arguments:
- coherency: float32 [16, 16, 8, 4096], P('band', None, None, 'base'), may hold values from -1.5 to 1.5
- observed: float32 [16, 8, 4096], P('band', None, 'base'), may hold values from -6 to 6
- jones_deviation: float32 [16, 16, 8, 512], P('band', None, None, 'base'), may hold values from -1.8 to 1.8
- antenna_first: int32 [4096], P('base'), may hold values from 0 to 511, as said below
- antenna_second: int32 [4096], P('base'), may hold values from 0 to 511, as said below
Outputs:
- jones: float32 [16, 16, 8, 512], P('band', None, None, 'base')
- residual: float32 [16, 8, 4096], P('band', None, 'base')
Inputs may be any that keep to these rules, and one draw needn't show every extreme that they name: `antenna_first`: every station is the first station of exactly 8 baselines. On every baseline antenna_second differs from antenna_first.
All inputs are finite; a program needn't handle non-finite values.
Results may differ from a plain program's by a relative error of at most 0.0003.
Values sent between devices are 32-bit elements; how exact they have to be, the bound alone decides.
A program may use at most 128 MiB of HBM per device.

v0:
```python
import jax
import jax.numpy as jnp
from jax import lax
from jax.sharding import PartitionSpec as P

ITERS = 3
step_gain = 1.2
penalty_gain = 0.25


def expand_matrix(packed):
    return [
        [(packed[..., 0, :], packed[..., 1, :]), (packed[..., 2, :], packed[..., 3, :])],
        [(packed[..., 4, :], packed[..., 5, :]), (packed[..., 6, :], packed[..., 7, :])],
    ]


def pack_matrix(matrix):
    return jnp.stack(
        [
            matrix[0][0][0],
            matrix[0][0][1],
            matrix[0][1][0],
            matrix[0][1][1],
            matrix[1][0][0],
            matrix[1][0][1],
            matrix[1][1][0],
            matrix[1][1][1],
        ],
        axis=-2,
    )


def complex_mul(first_term, second_term):
    return (
        first_term[0] * second_term[0] - first_term[1] * second_term[1],
        first_term[0] * second_term[1] + first_term[1] * second_term[0],
    )


def complex_add(first_term, second_term):
    return (first_term[0] + second_term[0], first_term[1] + second_term[1])


def element_of(matrix, i, j, adjoint):
    if adjoint:
        return (matrix[j][i][0], -matrix[j][i][1])
    return matrix[i][j]


def matrix_product(first_factor, second_factor, adjoint_first=False, adjoint_second=False):
    result_rows = []
    for i in range(2):
        row_items = []
        for j in range(2):
            row_items.append(
                complex_add(
                    complex_mul(
                        element_of(first_factor, i, 0, adjoint_first),
                        element_of(second_factor, 0, j, adjoint_second),
                    ),
                    complex_mul(
                        element_of(first_factor, i, 1, adjoint_first),
                        element_of(second_factor, 1, j, adjoint_second),
                    ),
                )
            )
        result_rows.append(row_items)
    return result_rows


def fit_basis(band_count):
    positions = (2.0 * jnp.arange(band_count, dtype=jnp.float32) + 1.0) / band_count - 1.0
    columns = []
    for power in range(4):
        vector = positions**power
        for earlier in columns:
            vector = vector - jnp.sum(earlier * vector) * earlier
        vector = vector / jnp.sqrt(jnp.sum(vector * vector))
        columns.append(vector)
    return jnp.stack(columns, axis=1)


def local_gradients(
    leading_rows, trailing_rows, coherency, observed, antenna_first, antenna_second, station_number
):
    leading_jones = expand_matrix(leading_rows)
    trailing_jones = expand_matrix(trailing_rows)
    sky = expand_matrix(coherency)
    model = pack_matrix(
        matrix_product(leading_jones, matrix_product(sky, trailing_jones, adjoint_second=True))
    )
    residual = observed - jnp.sum(model, axis=1)
    resid_parts = expand_matrix(residual[:, None])
    gradient_leading = pack_matrix(
        matrix_product(resid_parts, matrix_product(trailing_jones, sky, adjoint_second=True))
    )
    gradient_trailing = pack_matrix(
        matrix_product(resid_parts, matrix_product(leading_jones, sky), adjoint_first=True)
    )
    shape_out = (coherency.shape[0], coherency.shape[1], 8, station_number)
    gradient_list = (
        jnp.zeros(shape_out, jnp.float32)
        .at[:, :, :, antenna_first]
        .add(gradient_leading)
        .at[:, :, :, antenna_second]
        .add(gradient_trailing)
    )
    return (gradient_list, residual)


def per_device(coherency, observed, jones_deviation, antenna_first, antenna_second):
    highest = lax.Precision.HIGHEST
    base_count = lax.axis_size("base")
    band_count = lax.axis_size("band")
    sub_dev = coherency.shape[0]
    base_dev = coherency.shape[-1]
    own_stations = jones_deviation.shape[-1]
    station_number = own_stations * base_count
    baseline_count = base_dev * base_count
    step_size = step_gain * station_number / baseline_count
    penalty = penalty_gain * baseline_count / station_number
    poly_basis = fit_basis(sub_dev * band_count)
    local_basis = lax.dynamic_slice_in_dim(poly_basis, lax.axis_index("band") * sub_dev, sub_dev, 0)
    identity = jnp.array([1.0, 0.0, 0.0, 0.0, 0.0, 0.0, 1.0, 0.0], dtype=jnp.float32)[:, None]
    jones_current = identity + jones_deviation
    jones_current = lax.all_gather(jones_current, "base", axis=3, tiled=True)
    consensus = jones_current
    dual_var = jnp.zeros_like(jones_current)
    residual = None
    for iteration in range(ITERS):
        leading_rows = jnp.take(jones_current, antenna_first, axis=3)
        trailing_rows = jnp.take(jones_current, antenna_second, axis=3)
        local_terms, residual = local_gradients(
            leading_rows,
            trailing_rows,
            coherency,
            observed,
            antenna_first,
            antenna_second,
            station_number,
        )
        station_gradients = lax.psum(local_terms, "base")
        jones_current = jones_current + step_size * (
            station_gradients - dual_var - penalty * (jones_current - consensus)
        )
        if iteration + 1 < ITERS:
            target = jones_current + dual_var / penalty
            partial_fit = jnp.einsum("fm,fkcs->mkcs", local_basis, target, precision=highest)
            coefficients = lax.psum(partial_fit, "band")
            consensus = jnp.einsum("fm,mkcs->fkcs", local_basis, coefficients, precision=highest)
            dual_var = dual_var + penalty * (jones_current - consensus)
    jones_current = lax.dynamic_slice_in_dim(
        jones_current, lax.axis_index("base") * own_stations, own_stations, 3
    )
    return (jones_current, residual)


def solution(mesh):
    return jax.shard_map(
        per_device,
        mesh=mesh,
        in_specs=(
            P("band", None, None, "base"),
            P("band", None, "base"),
            P("band", None, None, "base"),
            P("base"),
            P("base"),
        ),
        out_specs=(P("band", None, None, "base"), P("band", None, "base")),
        check_vma=False,
    )
```

profile of v0, /device:TPU:0, one launch (start us, length us, event | category | flops | bytes accessed | tf_op | source)
XLA Modules:
  0.0 1139.3 jit_solution(16276159739745969013)
XLA Ops:
  19.4 120.1 %all-gather.2.cloned.1.call-done = f32[8,16,8,512]{1,2,0,3:T(8,128)} async-done(((f32[8,16,8,32]{1,2,0,3:T(8,128)}), f32[8,16,8,512]{1,2,0,3:T(8,128)}) %all-gather.2.cloned.1.call-update) | async-done | bytes 2097168 | tf_op jit(solution)/shard_map/all_gather | solution.py:127
  139.5 11.4 copy.497
  150.9 10.6 gather_fusion
  168.6 10.6 gather_fusion.1
  179.3 7.6 copy.501
  228.2 7.5 copy.527
  240.1 7.7 copy.536
  254.8 39.8 %scatter_fusion = f32[8,16,8,512]{1,2,3,0:T(8,128)} fusion(f32[8,16,8,512]{1,2,3,0:T(8,128)} %broadcast.414.clone, s32[256]{0:T(256)S(1)} %copy-done.42, f32[256,8,16,8]{2,3,1,0:T(8,128)} %copy.527), kind=kCustom, calls=%fused_computation.6 | custom fusion | flops 262144 | bytes 3146752 | tf_op jit(solution)/shard_map/scatter-add | solution.py:105
  294.7 39.9 %scatter_fusion.1 = f32[8,16,8,512]{1,2,3,0:T(8,128)} fusion(f32[8,16,8,512]{1,2,3,0:T(8,128)} %scatter_fusion, s32[256]{0:T(256)S(1)} %copy-done.38, f32[256,8,16,8]{2,3,1,0:T(8,128)} %copy.536), kind=kCustom, calls=%fused_computation.7 | custom fusion | flops 262144 | bytes 3146752 | tf_op jit(solution)/shard_map/scatter-add | solution.py:107
  334.6 9.7 copy.537
  350.6 12.2 %copy.540 = f32[8,16,8,512]{3,0,2,1:T(8,128)} copy(f32[8,16,8,512]{1,2,0,3:T(8,128)} %all-gather.2.cloned.1.call-done) | data formatting | bytes 4194304 | tf_op jit(solution)/shard_map/all_gather | solution.py:127
  362.8 78.2 %all-reduce.6.cloned.1.call-done = f32[8,16,8,512]{3,0,2,1:T(8,128)} async-done(((f32[8,16,8,512]{3,0,2,1:T(8,128)}), f32[8,16,8,512]{3,0,2,1:T(8,128)}) %all-reduce.6.cloned.1.call-update) | async-done | bytes 2097168 | tf_op jit(solution)/shard_map/psum | solution.py:143
  443.8 7.8 copy.541
  451.6 10.8 gather_fusion.2
  462.4 10.8 gather_fusion.3
  481.7 7.5 copy.544
  551.3 7.5 copy.563
  571.5 7.7 copy.572
  586.2 39.8 %scatter_fusion.2 = f32[8,16,8,512]{1,2,3,0:T(8,128)} fusion(f32[8,16,8,512]{1,2,3,0:T(8,128)} %broadcast.414.clone.1, s32[256]{0:T(256)S(1)} %copy-done.43, f32[256,8,16,8]{2,3,1,0:T(8,128)} %copy.563), kind=kCustom, calls=%fused_computation.8 | custom fusion | flops 262144 | bytes 3146752 | tf_op jit(solution)/shard_map/scatter-add | solution.py:105
  626.0 39.8 %scatter_fusion.3 = f32[8,16,8,512]{1,2,3,0:T(8,128)} fusion(f32[8,16,8,512]{1,2,3,0:T(8,128)} %scatter_fusion.2, s32[256]{0:T(256)S(1)} %copy-done.39, f32[256,8,16,8]{2,3,1,0:T(8,128)} %copy.572), kind=kCustom, calls=%fused_computation.9 | custom fusion | flops 262144 | bytes 3146752 | tf_op jit(solution)/shard_map/scatter-add | solution.py:107
  665.8 9.7 copy.573
  686.7 86.7 %all-reduce.8.cloned.1.call-done = f32[8,16,8,512]{3,0,2,1:T(8,128)} async-done(((f32[8,16,8,512]{3,0,2,1:T(8,128)}), f32[8,16,8,512]{3,0,2,1:T(8,128)}) %all-reduce.8.cloned.1.call-update) | async-done | bytes 2097168 | tf_op jit(solution)/shard_map/psum | solution.py:143
  773.5 41.6 %all-reduce.10.cloned.1.call-done = f32[4,16,8,512]{3,0,2,1:T(4,128)} async-done(((f32[4,16,8,512]{3,0,2,1:T(4,128)}), f32[4,16,8,512]{3,0,2,1:T(4,128)}) %all-reduce.10.cloned.1.call-update) | async-done | bytes 1048592 | tf_op jit(solution)/shard_map/psum | solution.py:150
  821.1 7.8 copy.574
  828.8 10.8 gather_fusion.4
  839.6 10.8 gather_fusion.5
  912.8 8.4 copy.596
  926.1 7.5 copy.605
  940.7 39.8 %scatter_fusion.4 = f32[8,16,8,512]{1,2,3,0:T(8,128)} fusion(f32[8,16,8,512]{1,2,3,0:T(8,128)} %broadcast.414, s32[256]{0:T(256)S(1)} %copy-done.44, f32[256,8,16,8]{2,3,1,0:T(8,128)} %copy.596), kind=kCustom, calls=%fused_computation.10 | custom fusion | flops 262144 | bytes 3146752 | tf_op jit(solution)/shard_map/scatter-add | solution.py:105
  980.5 39.8 %scatter_fusion.5 = f32[8,16,8,512]{1,2,3,0:T(8,128)} fusion(f32[8,16,8,512]{1,2,3,0:T(8,128)} %scatter_fusion.4, s32[256]{0:T(256)S(1)} %copy-done.40, f32[256,8,16,8]{2,3,1,0:T(8,128)} %copy.605), kind=kCustom, calls=%fused_computation.11 | custom fusion | flops 262144 | bytes 3146752 | tf_op jit(solution)/shard_map/scatter-add | solution.py:107
  1020.3 10.1 copy.606
  1036.3 92.8 %all-reduce.12.cloned.1.call-done = f32[8,16,8,512]{3,0,2,1:T(8,128)} async-done(((f32[8,16,8,512]{3,0,2,1:T(8,128)}), f32[8,16,8,512]{3,0,2,1:T(8,128)}) %all-reduce.12.cloned.1.call-update) | async-done | bytes 2097168 | tf_op jit(solution)/shard_map/psum | solution.py:143
  (305 shorter events, 267.1 us)
Async XLA Ops:
  7.2 132.3 %all-gather.2.cloned.1.call-start = ((), (), s32[]{:S(2)}) async-start(), calls=%async_computation | async-start | bytes 17825792 | tf_op jit(solution)/shard_map/all_gather | solution.py:127
  10.2 430.8 %all-reduce.6.cloned.1.call-start = ((), (), s32[]{:S(2)}) async-start(), calls=%async_computation.1 | async-start | bytes 4194304 | tf_op jit(solution)/shard_map/psum | solution.py:143
  11.5 187.3 %copy-start.13 = (f32[8,8,256]{1,0,2:T(8,128)}, f32[8,8,256]{1,0,2:T(8,128)S(1)}, u32[]{:S(2)}) copy-start(f32[8,8,256]{1,0,2:T(8,128)S(1)} %copy.510) | copy-start | bytes 196612
  12.3 138.6 %copy-start.45 = (s32[1024]{0:T(1024)}, s32[1024]{0:T(1024)S(1)}, u32[]{:S(2)}) copy-start(s32[1024]{0:T(1024)S(1)} %pad_clamp_fusion.1) | copy-start | bytes 12292
  12.9 155.8 %copy-start.46 = (s32[1024]{0:T(1024)}, s32[1024]{0:T(1024)S(1)}, u32[]{:S(2)}) copy-start(s32[1024]{0:T(1024)S(1)} %pad_clamp_fusion) | copy-start | bytes 12292
  13.6 173.3 %copy-start.50 = (pred[256]{0:T(512)(128)(4,1)}, pred[256]{0:T(512)(128)(4,1)S(1)}, u32[]{:S(2)}) copy-start(pred[256]{0:T(512)(128)(4,1)S(1)} %get-tuple-element.206) | copy-start | bytes 772
  13.6 174.7 %copy-start.47 = (pred[256]{0:T(512)(128)(4,1)}, pred[256]{0:T(512)(128)(4,1)S(1)}, u32[]{:S(2)}) copy-start(pred[256]{0:T(512)(128)(4,1)S(1)} %get-tuple-element.205) | copy-start | bytes 772
  19.3 198.3 %copy-start.5 = (f32[8,16,1,256]{3,2,1,0:T(1,128)}, f32[8,16,1,256]{3,2,1,0:T(1,128)S(1)}, u32[]{:S(2)}) copy-start(f32[8,16,1,256]{3,2,1,0:T(1,128)S(1)} %get-tuple-element.140) | copy-start | bytes 393220
  19.3 198.3 %copy-start.7 = (f32[8,16,1,256]{3,2,1,0:T(1,128)}, f32[8,16,1,256]{3,2,1,0:T(1,128)S(1)}, u32[]{:S(2)}) copy-start(f32[8,16,1,256]{3,2,1,0:T(1,128)S(1)} %get-tuple-element.142) | copy-start | bytes 393220
  19.4 198.3 %copy-start.9 = (f32[8,16,1,256]{3,2,1,0:T(1,128)}, f32[8,16,1,256]{3,2,1,0:T(1,128)S(1)}, u32[]{:S(2)}) copy-start(f32[8,16,1,256]{3,2,1,0:T(1,128)S(1)} %get-tuple-element.145) | copy-start | bytes 393220
  19.4 198.3 %copy-start.11 = (f32[8,16,1,256]{3,2,1,0:T(1,128)}, f32[8,16,1,256]{3,2,1,0:T(1,128)S(1)}, u32[]{:S(2)}) copy-start(f32[8,16,1,256]{3,2,1,0:T(1,128)S(1)} %get-tuple-element.146) | copy-start | bytes 393220
  19.4 199.8 %copy-start.3 = (f32[8,16,1,256]{3,2,1,0:T(1,128)}, f32[8,16,1,256]{3,2,1,0:T(1,128)S(1)}, u32[]{:S(2)}) copy-start(f32[8,16,1,256]{3,2,1,0:T(1,128)S(1)} %get-tuple-element.147) | copy-start | bytes 393220
  200.2 11.5 %copy-start.15 = (f32[8,16,8,256]{3,1,2,0:T(8,128)S(1)}, f32[8,16,8,256]{3,1,2,0:T(8,128)}, u32[]{:S(2)}) copy-start(f32[8,16,8,256]{3,1,2,0:T(8,128)} %copy-done.14) | copy-start | bytes 3145732
  247.8 46.9 %copy-start.38 = (s32[256]{0:T(256)S(1)}, s32[256]{0:T(256)}, u32[]{:S(2)}) copy-start(s32[256]{0:T(256)} %copy-done.37) | copy-start | bytes 3076
  344.3 429.2 %all-reduce.8.cloned.1.call-start = ((), (), s32[]{:S(2)}) async-start(), calls=%async_computation.2 | async-start | bytes 4194304 | tf_op jit(solution)/shard_map/psum | solution.py:143
  443.8 240.0 %copy-start.2 = (f32[8,16,8,512]{3,0,2,1:T(8,128)}, f32[8,16,8,512]{3,0,2,1:T(8,128)S(1)}, u32[]{:S(2)}) copy-start(f32[8,16,8,512]{3,0,2,1:T(8,128)S(1)} %multiply_add_fusion) | copy-start | bytes 6291460
  451.6 28.7 %copy-start.51 = (pred[256]{0:T(512)(128)(4,1)S(1)}, pred[256]{0:T(512)(128)(4,1)}, u32[]{:S(2)}) copy-start(pred[256]{0:T(512)(128)(4,1)} %copy-done.50) | copy-start | bytes 772
  473.2 16.0 %copy-start.48 = (pred[256]{0:T(512)(128)(4,1)S(1)}, pred[256]{0:T(512)(128)(4,1)}, u32[]{:S(2)}) copy-start(pred[256]{0:T(512)(128)(4,1)} %copy-done.47) | copy-start | bytes 772
  579.1 46.9 %copy-start.39 = (s32[256]{0:T(256)S(1)}, s32[256]{0:T(256)}, u32[]{:S(2)}) copy-start(s32[256]{0:T(256)} %copy-done.37) | copy-start | bytes 3076
  675.5 139.5 %all-reduce.10.cloned.1.call-start = ((), (), s32[]{:S(2)}) async-start(), calls=%async_computation.3 | async-start | bytes 2097152 | tf_op jit(solution)/shard_map/psum | solution.py:150
  683.8 145.0 %copy-start.35 = (f32[16,4]{0,1:T(4,128)}, f32[16,4]{0,1:T(4,128)S(1)}, u32[]{:S(2)}) copy-start(f32[16,4]{0,1:T(4,128)S(1)} %pad_maximum_fusion) | copy-start | bytes 772
  686.7 344.7 %all-reduce.14.cloned.1.call-start = ((), (), s32[]{:S(2)}) async-start(), calls=%async_computation.5 | async-start | bytes 2097152 | tf_op jit(solution)/shard_map/psum | solution.py:150
  828.8 27.8 %copy-start.52 = (pred[256]{0:T(512)(128)(4,1)S(1)}, pred[256]{0:T(512)(128)(4,1)}, u32[]{:S(2)}) copy-start(pred[256]{0:T(512)(128)(4,1)} %copy-done.50) | copy-start | bytes 772
  850.4 13.0 %copy-start.49 = (pred[256]{0:T(512)(128)(4,1)S(1)}, pred[256]{0:T(512)(128)(4,1)}, u32[]{:S(2)}) copy-start(pred[256]{0:T(512)(128)(4,1)} %copy-done.47) | copy-start | bytes 772
  900.9 228.2 %all-reduce.12.cloned.1.call-start = ((), (), s32[]{:S(2)}) async-start(), calls=%async_computation.4 | async-start | bytes 4194304 | tf_op jit(solution)/shard_map/psum | solution.py:143
  908.7 12.5 %copy-start.33 = (f32[8,1,1,256]{3,0,2,1:T(8,128)S(1)}, f32[8,1,1,256]{3,0,2,1:T(8,128)}, u32[]{:S(2)}) copy-start(f32[8,1,1,256]{3,0,2,1:T(8,128)} %copy.581) | copy-start | bytes 24580
  908.7 12.5 %copy-start.19 = (f32[8,1,1,256]{3,0,2,1:T(8,128)S(1)}, f32[8,1,1,256]{3,0,2,1:T(8,128)}, u32[]{:S(2)}) copy-start(f32[8,1,1,256]{3,0,2,1:T(8,128)} %copy.582) | copy-start | bytes 24580
  908.7 12.5 %copy-start.25 = (f32[8,256]{1,0:T(8,128)S(1)}, f32[8,256]{1,0:T(8,128)}, u32[]{:S(2)}) copy-start(f32[8,256]{1,0:T(8,128)} %bitcast_negate_fusion) | copy-start | bytes 24580
  908.7 12.5 %copy-start.26 = (f32[8,256]{1,0:T(8,128)S(1)}, f32[8,256]{1,0:T(8,128)}, u32[]{:S(2)}) copy-start(f32[8,256]{1,0:T(8,128)} %bitcast_negate_fusion.2) | copy-start | bytes 24580
  933.6 46.9 %copy-start.40 = (s32[256]{0:T(256)S(1)}, s32[256]{0:T(256)}, u32[]{:S(2)}) copy-start(s32[256]{0:T(256)} %copy-done.37) | copy-start | bytes 3076
  1020.3 11.2 copy-start.1
  1020.3 11.2 copy-start.36
  (28 other events, 147.5 us)
Sparse Core Ops, SparseCore 0:
  10.3 129.1 all-gather.1
  344.4 96.5 all-reduce.5
  675.6 97.8 all-reduce.7
  775.6 39.3 all-reduce.9
  901.0 40.0 all-reduce.13
  1030.6 98.4 all-reduce.11
where the time goes:
time: 1150 us; the launch traced here: 1140 us
  waiting for transfers between devices  419 us (36%)
  local copies, waits for them, and re-layouts  357 us (31%)
  other arithmetic  324 us (28%)
  between operations  19.6 us (2%)
  matrix products  18.7 us (2%)
    psum x3, waiting for transfers between devices, per_device(): station_gradients = lax.psum(local_terms, 'base')  258 us
    scatter-add x6, other arithmetic, local_gradients(): gradient_list = jnp.zeros(shape_out, jnp.float32).at[:, :, :, antenna_fir...  239 us
    all_gather x1, waiting for transfers between devices, per_device(): jones_current = lax.all_gather(jones_current, 'base', axis=3, tiled=True)  120 us
    another operation x12, local copies, waits for them, and re-layouts, pack_matrix(): jnp.stack([matrix[0][0][0], matrix[0][0][1], matrix[0][1][0], matrix[0][1...  61.1 us
    gather x6, local copies, waits for them, and re-layouts, per_device(): trailing_rows = jnp.take(jones_current, antenna_second, axis=3)  53.9 us
    gather x6, local copies, waits for them, and re-layouts, per_device(): leading_rows = jnp.take(jones_current, antenna_first, axis=3)  52.7 us
    psum x2, waiting for transfers between devices, per_device(): coefficients = lax.psum(partial_fit, 'band')  41.6 us
    scatter-add x3, local copies, waits for them, and re-layouts, local_gradients(): gradient_list = jnp.zeros(shape_out, jnp.float32).at[:, :, :, antenna_fir...  29.5 us
  transfers between devices with their start and end apart: 6, of which 5 were waited for; matrix products, arithmetic and copies ran while one was open for 15% of the time, Pallas kernels for 0%

commit v1 on v0

--- a/solution.py
+++ b/solution.py
@@ -140,7 +140,7 @@
             antenna_second,
             station_number,
         )
-        station_gradients = lax.psum(local_terms, "base")
+        station_gradients = jnp.sum(lax.all_gather(local_terms, "base"), axis=0)
         jones_current = jones_current + step_size * (
             station_gradients - dual_var - penalty * (jones_current - consensus)
         )

time: 1150 us -> 1400 us (1.22)
  waiting for transfers between devices: 419 us -> 614 us
  other arithmetic: 324 us -> 372 us
    all_gather x0 -> x3, waiting for transfers between devices: none -> 466 us  [per_device(): station_gradients = jnp.sum(lax.all_gather(local_terms, 'base'), axis=0)]
    psum x3 -> x0, waiting for transfers between devices: 258 us -> none  [per_device(): station_gradients = lax.psum(local_terms, 'base')]
    reduce_sum x0 -> x3, other arithmetic: none -> 42.8 us  [per_device(): station_gradients = jnp.sum(lax.all_gather(local_terms, 'base'), axis=0)]
  transfers between devices with their start and end apart: 6 -> 6, of which waited for: 5 -> 5; matrix products, arithmetic and copies ran while one was open for 15% -> 14% of each run, Pallas kernels for 0% -> 0%
where the time goes in v1:
time: 1400 us; the launch traced here: 1390 us
  waiting for transfers between devices  614 us (44%)
  other arithmetic  372 us (27%)
  local copies, waits for them, and re-layouts  361 us (26%)
  matrix products  20.1 us (1%)
  between operations  19.4 us (1%)
    all_gather x3, waiting for transfers between devices, per_device(): station_gradients = jnp.sum(lax.all_gather(local_terms, 'base'), axis=0)  466 us
    scatter-add x6, other arithmetic, local_gradients(): gradient_list = jnp.zeros(shape_out, jnp.float32).at[:, :, :, antenna_fir...  239 us
    all_gather x1, waiting for transfers between devices, per_device(): jones_current = lax.all_gather(jones_current, 'base', axis=3, tiled=True)  120 us
    another operation x12, local copies, waits for them, and re-layouts, pack_matrix(): jnp.stack([matrix[0][0][0], matrix[0][0][1], matrix[0][1][0], matrix[0][1...  61.5 us
    gather x6, local copies, waits for them, and re-layouts, per_device(): leading_rows = jnp.take(jones_current, antenna_first, axis=3)  54.5 us
    gather x6, local copies, waits for them, and re-layouts, per_device(): trailing_rows = jnp.take(jones_current, antenna_second, axis=3)  52.1 us
    reduce_sum x3, other arithmetic, per_device(): station_gradients = jnp.sum(lax.all_gather(local_terms, 'base'), axis=0)  42.8 us
    scatter-add x3, local copies, waits for them, and re-layouts, local_gradients(): gradient_list = jnp.zeros(shape_out, jnp.float32).at[:, :, :, antenna_fir...  33.6 us
  transfers between devices with their start and end apart: 6, of which 5 were waited for; matrix products, arithmetic and copies ran while one was open for 14% of the time, Pallas kernels for 0%

profile of v1, /device:TPU:0, one launch (start us, length us, event | category | flops | bytes accessed | tf_op | source)
XLA Modules:
  0.0 1387.2 jit_solution(1346328054872452884)
XLA Ops:
  19.3 120.2 %all-gather.8.cloned.1.call-done = f32[8,16,8,512]{1,2,0,3:T(8,128)} async-done(((f32[8,16,8,32]{1,2,0,3:T(8,128)}), f32[8,16,8,512]{1,2,0,3:T(8,128)}) %all-gather.8.cloned.1.call-update) | async-done | bytes 2097168 | tf_op jit(solution)/shard_map/all_gather | solution.py:127
  139.5 11.4 copy.509
  150.9 10.7 gather_fusion
  168.7 10.7 gather_fusion.1
  228.7 7.6 copy.548
  240.2 7.9 copy.539
  255.2 39.8 %scatter_fusion = f32[8,16,8,512]{1,2,3,0:T(8,128)} fusion(f32[8,16,8,512]{1,2,3,0:T(8,128)} %broadcast.414.clone, s32[256]{0:T(256)S(1)} %copy-done.53, f32[256,8,16,8]{2,3,1,0:T(8,128)} %copy.539), kind=kCustom, calls=%fused_computation.6 | custom fusion | flops 262144 | bytes 3146752 | tf_op jit(solution)/shard_map/scatter-add | solution.py:105
  295.0 39.9 %scatter_fusion.1 = f32[8,16,8,512]{1,2,3,0:T(8,128)} fusion(f32[8,16,8,512]{1,2,3,0:T(8,128)} %scatter_fusion, s32[256]{0:T(256)S(1)} %copy-done.49, f32[256,8,16,8]{2,3,1,0:T(8,128)} %copy.548), kind=kCustom, calls=%fused_computation.7 | custom fusion | flops 262144 | bytes 3146752 | tf_op jit(solution)/shard_map/scatter-add | solution.py:107
  334.9 11.1 copy.549
  346.1 12.9 copy.554
  359.0 153.5 %all-gather.10.cloned.1.call-done = f32[128,16,8,512]{3,2,1,0:T(8,128)} async-done(((f32[8,16,8,512]{3,2,1,0:T(8,128)}), f32[128,16,8,512]{3,2,1,0:T(8,128)}) %all-gather.10.cloned.1.call-update) | async-done | bytes 33554448 | tf_op jit(solution)/shard_map/all_gather | solution.py:143
  512.5 14.1 %reduce_sum.140 = f32[8,16,8,512]{3,2,1,0:T(8,128)} reduce(f32[16,8,16,8,512]{4,3,2,1,0:T(8,128)} %bitcast.82, f32[]{:T(128)} %constant.23.clone.1), dimensions={0}, to_apply=%region_3.5 | reduce | flops 7864320 | bytes 35651588 | tf_op jit(solution)/shard_map/reduce_sum | solution.py:143
  530.9 7.7 copy.555
  538.6 10.8 gather_fusion.3
  549.4 10.8 gather_fusion.2
  655.8 7.7 copy.577
  670.7 39.8 %scatter_fusion.2 = f32[8,16,8,512]{1,2,3,0:T(8,128)} fusion(f32[8,16,8,512]{1,2,3,0:T(8,128)} %broadcast.414.clone.1, s32[256]{0:T(256)S(1)} %copy-done.54, f32[256,8,16,8]{2,3,1,0:T(8,128)} %copy.577), kind=kCustom, calls=%fused_computation.8 | custom fusion | flops 262144 | bytes 3146752 | tf_op jit(solution)/shard_map/scatter-add | solution.py:105
  710.5 39.9 %scatter_fusion.3 = f32[8,16,8,512]{1,2,3,0:T(8,128)} fusion(f32[8,16,8,512]{1,2,3,0:T(8,128)} %scatter_fusion.2, s32[256]{0:T(256)S(1)} %copy-done.50, f32[256,8,16,8]{2,3,1,0:T(8,128)} %copy.586), kind=kCustom, calls=%fused_computation.9 | custom fusion | flops 262144 | bytes 3146752 | tf_op jit(solution)/shard_map/scatter-add | solution.py:107
  750.4 11.1 copy.587
  779.0 150.7 %all-gather.12.cloned.1.call-done = f32[128,16,8,512]{3,2,1,0:T(8,128)} async-done(((f32[8,16,8,512]{3,2,1,0:T(8,128)}), f32[128,16,8,512]{3,2,1,0:T(8,128)}) %all-gather.12.cloned.1.call-update) | async-done | bytes 33554448 | tf_op jit(solution)/shard_map/all_gather | solution.py:143
  929.7 14.7 %reduce_sum.142 = f32[8,16,8,512]{3,2,1,0:T(8,128)} reduce(f32[16,8,16,8,512]{4,3,2,1,0:T(8,128)} %bitcast.80, f32[]{:T(128)} %constant.23.clone.1), dimensions={0}, to_apply=%region_7.9 | reduce | flops 7864320 | bytes 35651588 | tf_op jit(solution)/shard_map/reduce_sum | solution.py:143
  944.4 27.6 %all-reduce.3.cloned.1.call-done = f32[4,16,8,512]{3,0,2,1:T(4,128)} async-done(((f32[4,16,8,512]{3,0,2,1:T(4,128)}), f32[4,16,8,512]{3,0,2,1:T(4,128)}) %all-reduce.3.cloned.1.call-update) | async-done | bytes 1048592 | tf_op jit(solution)/shard_map/psum | solution.py:150
  979.2 7.7 copy.590
  986.9 10.8 gather_fusion.5
  997.7 10.8 gather_fusion.4
  1015.0 7.8 copy.591
  1075.0 8.4 copy.621
  1103.1 39.8 %scatter_fusion.4 = f32[8,16,8,512]{1,2,3,0:T(8,128)} fusion(f32[8,16,8,512]{1,2,3,0:T(8,128)} %broadcast.414, s32[256]{0:T(256)S(1)} %copy-done.55, f32[256,8,16,8]{2,3,1,0:T(8,128)} %copy.612), kind=kCustom, calls=%fused_computation.10 | custom fusion | flops 262144 | bytes 3146752 | tf_op jit(solution)/shard_map/scatter-add | solution.py:105
  1142.8 39.9 %scatter_fusion.5 = f32[8,16,8,512]{1,2,3,0:T(8,128)} fusion(f32[8,16,8,512]{1,2,3,0:T(8,128)} %scatter_fusion.4, s32[256]{0:T(256)S(1)} %copy-done.51, f32[256,8,16,8]{2,3,1,0:T(8,128)} %copy.621), kind=kCustom, calls=%fused_computation.11 | custom fusion | flops 262144 | bytes 3146752 | tf_op jit(solution)/shard_map/scatter-add | solution.py:107
  1182.8 11.3 copy.622
  1199.9 162.3 %all-gather.14.cloned.1.call-done = f32[128,16,8,512]{3,2,1,0:T(8,128)} async-done(((f32[8,16,8,512]{3,2,1,0:T(8,128)}), f32[128,16,8,512]{3,2,1,0:T(8,128)}) %all-gather.14.cloned.1.call-update) | async-done | bytes 33554448 | tf_op jit(solution)/shard_map/all_gather | solution.py:143
  1362.2 14.1 %reduce_sum.153 = f32[8,16,8,512]{3,2,1,0:T(8,128)} reduce(f32[16,8,16,8,512]{4,3,2,1,0:T(8,128)} %bitcast.81, f32[]{:T(128)} %constant.23.clone.1), dimensions={0}, to_apply=%region_21.23 | reduce | flops 7864320 | bytes 35651588 | tf_op jit(solution)/shard_map/reduce_sum | solution.py:143
  (329 shorter events, 294.3 us)
Async XLA Ops:
  7.2 132.3 %all-gather.8.cloned.1.call-start = ((), (), s32[]{:S(2)}) async-start(), calls=%async_computation | async-start | bytes 17825792 | tf_op jit(solution)/shard_map/all_gather | solution.py:127
  10.2 502.3 %all-gather.10.cloned.1.call-start = ((), (), s32[]{:S(2)}) async-start(), calls=%async_computation.3 | async-start | bytes 35651584 | tf_op jit(solution)/shard_map/all_gather | solution.py:143
  11.5 187.1 %copy-start.13 = (f32[8,8,256]{1,0,2:T(8,128)}, f32[8,8,256]{1,0,2:T(8,128)S(1)}, u32[]{:S(2)}) copy-start(f32[8,8,256]{1,0,2:T(8,128)S(1)} %copy.522) | copy-start | bytes 196612
  12.3 138.6 %copy-start.56 = (s32[1024]{0:T(1024)}, s32[1024]{0:T(1024)S(1)}, u32[]{:S(2)}) copy-start(s32[1024]{0:T(1024)S(1)} %pad_clamp_fusion.1) | copy-start | bytes 12292
  12.9 155.8 %copy-start.57 = (s32[1024]{0:T(1024)}, s32[1024]{0:T(1024)S(1)}, u32[]{:S(2)}) copy-start(s32[1024]{0:T(1024)S(1)} %pad_clamp_fusion) | copy-start | bytes 12292
  13.6 173.1 %copy-start.58 = (pred[256]{0:T(512)(128)(4,1)}, pred[256]{0:T(512)(128)(4,1)S(1)}, u32[]{:S(2)}) copy-start(pred[256]{0:T(512)(128)(4,1)S(1)} %get-tuple-element.206) | copy-start | bytes 772
  13.6 174.5 %copy-start.61 = (pred[256]{0:T(512)(128)(4,1)}, pred[256]{0:T(512)(128)(4,1)S(1)}, u32[]{:S(2)}) copy-start(pred[256]{0:T(512)(128)(4,1)S(1)} %get-tuple-element.205) | copy-start | bytes 772
  19.3 198.3 %copy-start.5 = (f32[8,16,1,256]{3,2,1,0:T(1,128)}, f32[8,16,1,256]{3,2,1,0:T(1,128)S(1)}, u32[]{:S(2)}) copy-start(f32[8,16,1,256]{3,2,1,0:T(1,128)S(1)} %get-tuple-element.140) | copy-start | bytes 393220
  19.3 198.3 %copy-start.7 = (f32[8,16,1,256]{3,2,1,0:T(1,128)}, f32[8,16,1,256]{3,2,1,0:T(1,128)S(1)}, u32[]{:S(2)}) copy-start(f32[8,16,1,256]{3,2,1,0:T(1,128)S(1)} %get-tuple-element.141) | copy-start | bytes 393220
  19.3 198.3 %copy-start.9 = (f32[8,16,1,256]{3,2,1,0:T(1,128)}, f32[8,16,1,256]{3,2,1,0:T(1,128)S(1)}, u32[]{:S(2)}) copy-start(f32[8,16,1,256]{3,2,1,0:T(1,128)S(1)} %get-tuple-element.142) | copy-start | bytes 393220
  19.3 198.3 %copy-start.11 = (f32[8,16,1,256]{3,2,1,0:T(1,128)}, f32[8,16,1,256]{3,2,1,0:T(1,128)S(1)}, u32[]{:S(2)}) copy-start(f32[8,16,1,256]{3,2,1,0:T(1,128)S(1)} %get-tuple-element.147) | copy-start | bytes 393220
  19.3 199.9 %copy-start.3 = (f32[8,16,1,256]{3,2,1,0:T(1,128)}, f32[8,16,1,256]{3,2,1,0:T(1,128)S(1)}, u32[]{:S(2)}) copy-start(f32[8,16,1,256]{3,2,1,0:T(1,128)S(1)} %get-tuple-element.146) | copy-start | bytes 393220
  222.5 13.8 copy-start.21
  222.5 13.8 copy-start.22
  222.5 13.8 copy-start.23
  222.5 13.8 copy-start.24
  222.5 13.8 copy-start.25
  248.1 46.9 %copy-start.49 = (s32[256]{0:T(256)S(1)}, s32[256]{0:T(256)}, u32[]{:S(2)}) copy-start(s32[256]{0:T(256)} %copy-done.48) | copy-start | bytes 3076
  346.0 583.7 %all-gather.12.cloned.1.call-start = ((), (), s32[]{:S(2)}) async-start(), calls=%async_computation.4 | async-start | bytes 35651584 | tf_op jit(solution)/shard_map/all_gather | solution.py:143
  530.9 245.2 %copy-start.2 = (f32[8,16,8,512]{3,0,2,1:T(8,128)}, f32[8,16,8,512]{3,0,2,1:T(8,128)S(1)}, u32[]{:S(2)}) copy-start(f32[8,16,8,512]{3,0,2,1:T(8,128)S(1)} %fusion.3) | copy-start | bytes 6291460
  538.6 27.9 %copy-start.62 = (pred[256]{0:T(512)(128)(4,1)S(1)}, pred[256]{0:T(512)(128)(4,1)}, u32[]{:S(2)}) copy-start(pred[256]{0:T(512)(128)(4,1)} %copy-done.61) | copy-start | bytes 772
  560.3 14.7 %copy-start.59 = (pred[256]{0:T(512)(128)(4,1)S(1)}, pred[256]{0:T(512)(128)(4,1)}, u32[]{:S(2)}) copy-start(pred[256]{0:T(512)(128)(4,1)} %copy-done.58) | copy-start | bytes 772
  607.9 14.1 %copy-start.19 = (f32[8,1,1,256]{2,0,3,1:T(8,128)S(1)}, f32[8,1,1,256]{2,0,3,1:T(8,128)}, u32[]{:S(2)}) copy-start(f32[8,1,1,256]{2,0,3,1:T(8,128)} %get-tuple-element.124) | copy-start | bytes 24580
  663.6 46.9 %copy-start.50 = (s32[256]{0:T(256)S(1)}, s32[256]{0:T(256)}, u32[]{:S(2)}) copy-start(s32[256]{0:T(256)} %copy-done.48) | copy-start | bytes 3076
  761.6 210.4 %all-reduce.3.cloned.1.call-start = ((), (), s32[]{:S(2)}) async-start(), calls=%async_computation.1 | async-start | bytes 2097152 | tf_op jit(solution)/shard_map/psum | solution.py:150
  776.1 195.9 %copy-start.46 = (f32[16,4]{0,1:T(4,128)}, f32[16,4]{0,1:T(4,128)S(1)}, u32[]{:S(2)}) copy-start(f32[16,4]{0,1:T(4,128)S(1)} %pad_maximum_fusion) | copy-start | bytes 772
  779.0 416.1 %all-reduce.5.cloned.1.call-start = ((), (), s32[]{:S(2)}) async-start(), calls=%async_computation.2 | async-start | bytes 2097152 | tf_op jit(solution)/shard_map/psum | solution.py:150
  986.9 27.9 %copy-start.63 = (pred[256]{0:T(512)(128)(4,1)S(1)}, pred[256]{0:T(512)(128)(4,1)}, u32[]{:S(2)}) copy-start(pred[256]{0:T(512)(128)(4,1)} %copy-done.61) | copy-start | bytes 772
  1008.5 14.2 %copy-start.60 = (pred[256]{0:T(512)(128)(4,1)S(1)}, pred[256]{0:T(512)(128)(4,1)}, u32[]{:S(2)}) copy-start(pred[256]{0:T(512)(128)(4,1)} %copy-done.58) | copy-start | bytes 772
  1054.3 308.0 %all-gather.14.cloned.1.call-start = ((), (), s32[]{:S(2)}) async-start(), calls=%async_computation.5 | async-start | bytes 35651584 | tf_op jit(solution)/shard_map/all_gather | solution.py:143
  1062.2 21.3 %copy-start.15 = (f32[8,16,8,256]{3,1,2,0:T(8,128)S(1)}, f32[8,16,8,256]{3,1,2,0:T(8,128)}, u32[]{:S(2)}) copy-start(f32[8,16,8,256]{3,1,2,0:T(8,128)} %copy-done.14) | copy-start | bytes 3145732
  1095.9 46.9 %copy-start.51 = (s32[256]{0:T(256)S(1)}, s32[256]{0:T(256)}, u32[]{:S(2)}) copy-start(s32[256]{0:T(256)} %copy-done.48) | copy-start | bytes 3076
  (38 other events, 277.7 us)
Sparse Core Ops, SparseCore 0:
  10.3 129.1 all-gather.7
  346.2 166.3 all-gather.9
  761.7 167.9 all-gather.11
  931.9 40.0 all-reduce.2
  1054.4 40.0 all-reduce.4
  1194.2 167.9 all-gather.13
